TPU v7x, 128 devices: a whole 4x4x4 slice. The times are simulated.
128 devices in a mesh: front: 8 (over z, core), grid: 16 (over y, x).
Axes of the slice: x: 4, y: 4, z: 4, core: 2. Of those that a mesh axis runs over, the one named last changes fastest.
Arguments:
- pivot_block: float32 [8, 512, 512], P('front'), as said below
- border: float32 [8, 8192, 512], P('front', 'grid'), may hold values from -0.9 to 0.9
- trailing: float32 [8, 8192, 8192], P('front', 'grid'), as said below
- dest_owner: int32 [8, 2560, 1], P('front', 'grid'), may hold values from 0 to 127; in each aligned block of 160 rows (0 to 159, 160 to 319, ..., all dimensions but the last counted through in order) at most 2 rows name the same one
- dest_slot: int32 [8, 2560], P('front', 'grid'), may hold values from 0 to 63
- row_map: int32 [8, 2560, 128], P('front', 'grid'), may hold values from 0 to 127, each once within a row
Outputs:
- pivot_factor: float32 [8, 512, 512], P('front')
- border_factor: float32 [8, 8192, 512], P('front', 'grid')
- ancestor_blocks: float32 [8192, 128, 128], P(('front', 'grid'))
Inputs may be any that keep to these rules, and one draw needn't show every extreme that they name: `pivot_block`: symmetric positive definite. `trailing`: Symmetric. `dest_owner`: in each aligned block of 160 entries no owner is named more than 2 times, a bound that some block reaches.
All inputs are finite; a program needn't handle non-finite values.
Results may differ from a plain program's by a relative error of at most 0.0001.
Values sent between devices are 32-bit elements; how exact they have to be, the bound alone decides.
A program may use at most 192 MiB of HBM per device.

v0:
```python
import jax
import jax.numpy as jnp
from jax import lax
from jax.sharding import PartitionSpec as P

BLK = 128
NB = 256
SLOTS = 64
precise = lax.Precision.HIGHEST


def factor_panels(corner, border_rows_in):
    first_factor = jnp.linalg.cholesky(corner[:NB, :NB])
    remainder = jnp.concatenate([corner[NB:, :NB], border_rows_in[:, :NB]], axis=0)
    solved = jax.scipy.linalg.solve_triangular(first_factor, remainder.T, lower=True).T
    pivot_rows = solved[:NB]
    border_rows = solved[NB:]
    updated_pivot = corner[NB:, NB:] - jnp.dot(pivot_rows, pivot_rows.T, precision=precise)
    updated_border = border_rows_in[:, NB:] - jnp.dot(border_rows, pivot_rows.T, precision=precise)
    second_factor = jnp.linalg.cholesky(updated_pivot)
    second_border = jax.scipy.linalg.solve_triangular(second_factor, updated_border.T, lower=True).T
    upper_half = jnp.concatenate([first_factor, jnp.zeros((NB, NB), jnp.float32)], axis=1)
    lower_half = jnp.concatenate([pivot_rows, second_factor], axis=1)
    return (
        jnp.concatenate([upper_half, lower_half], axis=0),
        jnp.concatenate([border_rows, second_border], axis=1),
    )


def subtract_outer(base_rows, left_rows, piece):
    return base_rows - jnp.einsum("rk,ck->rc", left_rows, piece, precision=precise)


def body(pivot_block, border, trailing, dest_owner, dest_slot, row_map):
    pivot_factor, border_factor = factor_panels(pivot_block[0], border[0])
    local_rows = trailing[0]
    schur_rows = local_rows
    for column_start in (0, NB):
        panel_cols = border_factor[:, column_start : column_start + NB]
        schur_rows = subtract_outer(
            schur_rows, panel_cols, lax.all_gather(panel_cols, "grid", axis=0, tiled=True)
        )
    group_size = lax.axis_size("grid")
    member = lax.axis_index("grid")
    per_dev = local_rows.shape[0] // BLK
    blocks_all = local_rows.shape[1] // BLK
    listed = dest_owner.shape[1]
    candidates = jnp.arange(per_dev * blocks_all, dtype=jnp.int32)
    local_block = candidates // blocks_all
    column_block = candidates % blocks_all
    true_column = column_block % per_dev * group_size + column_block // per_dev
    true_row = local_block * group_size + member
    usable = true_column <= true_row
    position = jnp.cumsum(usable.astype(jnp.int32)) - 1
    matches = (
        usable[None, :] & (position[None, :] == jnp.arange(listed, dtype=jnp.int32)[:, None])
    ).astype(jnp.float32)
    front_count = lax.axis_size("front")
    devices = front_count * group_size
    capacity = max(2, (listed + devices - 1) // devices)
    owner_id = dest_owner[0, :, 0]
    owner_hits = (owner_id[:, None] == jnp.arange(devices, dtype=jnp.int32)[None, :]).astype(
        jnp.int32
    )
    earlier = jnp.cumsum(owner_hits, axis=0) - owner_hits
    rank_in = jnp.sum(earlier * owner_hits, axis=1)
    buffer_place = owner_id * capacity + rank_in
    slot_hits = buffer_place[None, :] == jnp.arange(devices * capacity, dtype=jnp.int32)[:, None]
    sender = jnp.sum(
        slot_hits.astype(jnp.int32) * jnp.arange(listed, dtype=jnp.int32)[None, :], axis=1
    )
    filled = jnp.any(slot_hits, axis=1)
    selector = jnp.dot(slot_hits.astype(jnp.float32), matches, precision=precise)
    selector = selector.reshape(devices * capacity, per_dev, blocks_all)
    blocked = schur_rows.reshape(per_dev, BLK, blocks_all, BLK)
    picked = jnp.einsum("qkc,krcs->qrs", selector, blocked, precision=precise)
    row_order = row_map[0][sender]
    permuter = (row_order[:, :, None] == jnp.arange(BLK, dtype=jnp.int32)[None, None, :]).astype(
        jnp.float32
    )
    moved = jnp.einsum("qrs,qsx->qrx", permuter, picked, precision=precise)
    outgoing = moved.reshape(devices, capacity, BLK * BLK)
    slot_out = jnp.where(filled, dest_slot[0][sender], 0).reshape(devices, capacity)
    arrived, slot_in = (
        lax.all_to_all(outgoing, ("front", "grid"), split_axis=0, concat_axis=0, tiled=True),
        lax.all_to_all(slot_out, ("front", "grid"), split_axis=0, concat_axis=0, tiled=True),
    )
    arrived = arrived.reshape(devices * capacity, BLK * BLK)
    slot_in = slot_in.reshape(devices * capacity)
    chooser = (slot_in[:, None] == jnp.arange(SLOTS, dtype=jnp.int32)[None, :]).astype(jnp.float32)
    summed = jnp.einsum("rs,rx->sx", chooser, arrived, precision=precise)
    return (pivot_factor[None], border_factor[None], summed.reshape(SLOTS, BLK, BLK))


def solution(mesh):
    return jax.shard_map(
        body,
        mesh=mesh,
        in_specs=(
            P("front", None, None),
            P("front", "grid", None),
            P("front", "grid", None),
            P("front", "grid", None),
            P("front", "grid"),
            P("front", "grid", None),
        ),
        out_specs=(
            P("front", None, None),
            P("front", "grid", None),
            P(("front", "grid"), None, None),
        ),
        check_vma=False,
    )
```

profile of v0, /device:TPU:5, one launch (start us, length us, event | category | flops | bytes accessed | tf_op | source)
XLA Modules:
  0.0 670.3 jit_solution(7392036229213009177)
XLA Ops:
  7.3 1.6 copy.53
  9.1 11.7 %cholesky.130 = f32[128,128]{1,0:T(8,128)S(1)} custom-call(f32[128,128]{1,0:T(8,128)S(1)} %cholesky.194), custom_call_target="Cholesky" | custom-call | tf_op jit(solution)/shard_map/jit(cholesky)/cholesky | solution.py:13
  20.8 9.8 %custom-call.19 = f32[1,128,128]{1,2,0:T(8,128)S(1)} custom-call(f32[1,128,128]{2,1,0:T(8,128)S(1)} %get-tuple-element.65), custom_call_target="InvertDiagBlocksLowerTriangular" | custom-call | tf_op jit(solution)/shard_map/jit(cholesky)/cholesky | solution.py:13
  30.7 0.2 constant_dynamic-update-slice_fusion.3
  30.9 0.3 convolution_subtract_fusion.5
  31.1 11.7 %cholesky.147 = f32[128,128]{1,0:T(8,128)S(1)} custom-call(f32[128,128]{1,0:T(8,128)S(1)} %convolution_subtract_fusion.5), custom_call_target="Cholesky" | custom-call | tf_op jit(solution)/shard_map/jit(cholesky)/cholesky | solution.py:13
  42.9 0.6 compare_reduce_fusion.2
  44.8 0.7 fusion.20
  45.7 4.3 while.2
  45.9 0.6 fusion.76
  46.5 1.4 bitcast_dynamic-update-slice_fusion.4
  47.9 0.6 fusion.76
  48.5 1.4 bitcast_dynamic-update-slice_fusion.4
  49.9 19.7 %custom-call.16 = f32[2,128,128]{1,2,0:T(8,128)S(1)} custom-call(f32[2,128,128]{2,1,0:T(8,128)S(1)} %get-tuple-element.11), custom_call_target="InvertDiagBlocksLowerTriangular" | custom-call | tf_op jit(solution)/shard_map/jit(_solve_triangular)/triangular_solve | solution.py:15
  69.6 1.6 copy.55
  71.3 0.5 fusion.13
  71.8 0.5 convolution_subtract_fusion.1
  72.3 0.9 copy.56
  73.2 0.8 fusion.37
  74.0 1.1 maximum_bitcast_fusion.2
  75.1 0.8 slice.133
  76.0 0.4 convolution_subtract_fusion.3
  76.6 11.7 %cholesky.164 = f32[128,128]{1,0:T(8,128)S(1)} custom-call(f32[128,128]{1,0:T(8,128)S(1)} %cholesky.197), custom_call_target="Cholesky" | custom-call | tf_op jit(solution)/shard_map/jit(cholesky)/cholesky | solution.py:20
  88.4 9.8 %custom-call.20 = f32[1,128,128]{1,2,0:T(8,128)S(1)} custom-call(f32[1,128,128]{2,1,0:T(8,128)S(1)} %get-tuple-element.61), custom_call_target="InvertDiagBlocksLowerTriangular" | custom-call | tf_op jit(solution)/shard_map/jit(cholesky)/cholesky | solution.py:20
  98.2 0.3 fusion.34
  98.6 0.3 convolution_subtract_fusion.4
  98.9 11.7 %cholesky.181 = f32[128,128]{1,0:T(8,128)S(1)} custom-call(f32[128,128]{1,0:T(8,128)S(1)} %convolution_subtract_fusion.4), custom_call_target="Cholesky" | custom-call | tf_op jit(solution)/shard_map/jit(cholesky)/cholesky | solution.py:20
  110.7 0.6 compare_reduce_fusion
  111.3 0.6 compare_reduce_fusion.1
  113.2 12.1 %while.3 = (s32[]{:T(128)}, f32[256,256]{1,0:T(8,128)S(1)}, s32[2,2]{1,0:T(2,128)S(1)}, f32[2,128,128]{2,1,0:T(8,128)S(1)}, s32[]{:T(128)}) while((s32[]{:T(128)}, f32[256,256]{1,0:T(8,128)S(1)}, s32[2,2]{1,0:T(2,128)S(1)}, f32[2,128,128]{2,1,0:T(8,128)S(1)}, s32[]{:T(128)}) %tuple.61), condition=%wide.while_cond.1, body=%wide.while_body.1.sunk | while | flops 2 | bytes 131181 | solution.py:21
  121.5 0.6 fusion.77
  122.1 1.3 bitcast_dynamic-update-slice_fusion.5
  123.4 0.6 fusion.77
  124.0 1.3 bitcast_dynamic-update-slice_fusion.5
  125.3 19.7 %custom-call.17 = f32[2,128,128]{1,2,0:T(8,128)S(1)} custom-call(f32[2,128,128]{2,1,0:T(8,128)S(1)} %get-tuple-element.19), custom_call_target="InvertDiagBlocksLowerTriangular" | custom-call | tf_op jit(solution)/shard_map/jit(_solve_triangular)/triangular_solve | solution.py:21
  145.0 0.6 fusion.10
  145.6 0.4 fusion.15
  146.2 0.4 convolution_subtract_fusion.2
  146.6 1.4 fusion.33
  148.0 0.8 fusion.12
  149.2 0.2 fusion.28
  149.6 1.9 gather_fusion
  151.6 0.8 select_n.78
  152.4 10.8 %all-to-all-start = ((s32[128,1,2]{2,1,0:T(1,128)}), s32[128,1,2]{2,1,0:T(1,128)S(1)}, u32[]{:S(2)}, u32[]{:S(2)}) async-start(s32[128,1,2]{2,1,0:T(1,128)} %bitcast.26), calls=%async_computation | async-start | bytes 131072 | tf_op jit(solution)/shard_map/all_to_all | solution.py:86
  163.3 0.3 reduce-window.19
  163.7 0.7 gather_fusion.1
  164.6 0.3 fusion.21
  165.0 18.5 %fusion.56 = f32[512,8192]{1,0:T(8,128)} fusion(f32[8192,256]{1,0:T(8,128)} %all-gather.3.cloned.1.call-done, f32[768,256]{1,0:T(8,128)S(1)} %maximum_bitcast_fusion.2), kind=kOutput, calls=%fused_computation.134 | convolution fusion | flops 12884901888 | bytes 25690112 | tf_op jit(solution)/shard_map/rk,ck->rc/dot_general | solution.py:31
  183.5 39.6 %all-gather.5.cloned.1.call-done = f32[8192,256]{1,0:T(8,128)} async-done(((f32[512,256]{1,0:T(8,128)}), f32[8192,256]{1,0:T(8,128)}) %all-gather.5.cloned.1.call-update) | async-done | bytes 8388624 | tf_op jit(solution)/shard_map/all_gather | solution.py:41
  223.1 42.1 %fusion.3 = f32[64,8,64,128]{3,1,2,0:T(8,128)} fusion(f32[512,8192]{1,0:T(8,128)} %fusion.56, f32[1,512,8192]{2,1,0:T(8,128)} %param.9, f32[8192,256]{1,0:T(8,128)} %all-gather.5.cloned.1.call-done, f32[128,512]{0,1:T(8,128)S(1)} %fusion.33, f32[128,512]{0,1:T(8,128)S(1)} %copy.62), kind=kOutput, calls=%fused_computation.10 | convolution fusion | flops 12893421568 | bytes 59244544 | tf_op jit(solution)/shard_map/rk,ck->rc/dot_general | solution.py:31
  265.2 14.1 %copy.76 = f32[64,8,64,128]{3,2,1,0:T(8,128)} copy(f32[64,8,64,128]{3,1,2,0:T(8,128)} %fusion.3) | data formatting | bytes 33554432
  279.3 18.7 %fusion.6 = f32[256,128,128]{2,0,1:T(8,128)S(1)} fusion(f32[256,4,64,1]{0,2,3,1:T(8,128)S(1)} %bitcast.140, f32[4,128,64,128]{3,2,1,0:T(8,128)} %bitcast.130), kind=kOutput, calls=%fused_computation.14 | convolution fusion | flops 12884901888 | bytes 33816576 | tf_op jit(solution)/shard_map/qkc,krcs->qrs/dot_general | solution.py:76
  298.0 26.6 %fusion.4 = f32[256,128,128]{2,1,0:T(8,128)} fusion(f32[256,128,128]{2,0,1:T(8,128)S(1)} %fusion.6, s32[256,128]{1,0:T(8,128)S(1)} %gather_fusion.1), kind=kOutput, calls=%fused_computation.11 | convolution fusion | flops 6446645248 | bytes 33685504 | tf_op jit(solution)/shard_map/qrs,qsx->qrx/dot_general | solution.py:81
  324.6 19.8 %reshape.216 = f32[128,2,16384]{2,1,0:T(2,128)} reshape(f32[256,128,128]{2,1,0:T(8,128)} %fusion.4) | data formatting | bytes 33554432 | tf_op jit(solution)/shard_map/reshape | solution.py:82
  344.4 9.2 %all-to-all-start.1 = ((f32[128,2,16384]{2,1,0:T(2,128)}), f32[128,2,16384]{2,1,0:T(2,128)}, u32[]{:S(2)}, u32[]{:S(2)}) async-start(f32[128,2,16384]{2,1,0:T(2,128)} %reshape.216), calls=%async_computation.1 | async-start | bytes 33554432 | tf_op jit(solution)/shard_map/all_to_all | solution.py:85
  353.6 1.1 maximum_bitcast_fusion
  354.7 1.1 fusion.11
  355.8 0.5 broadcast.390
  356.4 0.8 reduce.13
  357.3 251.7 %all-to-all-done.1 = f32[128,2,16384]{2,1,0:T(2,128)} async-done(((f32[128,2,16384]{2,1,0:T(2,128)}), f32[128,2,16384]{2,1,0:T(2,128)}, u32[]{:S(2)}, u32[]{:S(2)}) %all-to-all-start.1) | async-done | bytes 16777248 | tf_op jit(solution)/shard_map/all_to_all | solution.py:85
  609.0 20.5 %reshape.217 = f32[256,16384]{1,0:T(8,128)} reshape(f32[128,2,16384]{2,1,0:T(2,128)} %all-to-all-done.1) | data formatting | bytes 33554432 | tf_op jit(solution)/shard_map/reshape | solution.py:88
  629.5 17.5 %copy.69 = f32[256,16384]{0,1:T(8,128)} copy(f32[256,16384]{1,0:T(8,128)} %reshape.217) | data formatting | bytes 33554432 | tf_op jit(solution)/shard_map/reshape | solution.py:88
  647.0 11.5 %fusion.43 = f32[64,128,128]{2,0,1:T(8,128)S(1)} fusion(f32[128,128,256]{2,1,0:T(8,128)} %bitcast.129, s32[256]{0:T(256)S(1)} %eq.86), kind=kOutput, calls=%fused_computation.86 | convolution fusion | flops 3221241856 | bytes 20972544 | tf_op jit(solution)/shard_map/rs,rx->sx/dot_general | solution.py:91
  658.5 4.4 copy.70
  (72 shorter events, 2.3 us)
Async XLA Ops:
  7.2 156.5 %copy-start = (s32[1,160,128]{2,1,0:T(8,128)S(1)}, s32[1,160,128]{2,1,0:T(8,128)}, u32[]{:S(2)}) copy-start(s32[1,160,128]{2,1,0:T(8,128)} %param.12) | copy-start | bytes 245764
  7.2 141.7 %copy-start.7 = (s32[1,160,1]{1,2,0:T(1,128)S(1)}, s32[1,160,1]{1,2,0:T(1,128)}, u32[]{:S(2)}) copy-start(s32[1,160,1]{1,2,0:T(1,128)} %param.10) | copy-start | bytes 1924
  7.2 142.4 %copy-start.2 = (s32[1,160]{1,0:T(1,128)S(1)}, s32[1,160]{1,0:T(1,128)}, u32[]{:S(2)}) copy-start(s32[1,160]{1,0:T(1,128)} %param.11) | copy-start | bytes 1924
  7.2 157.7 %all-gather.3.cloned.1.call-start = ((), (), s32[]{:S(2)}) async-start(), calls=%async_computation.2 | async-start | bytes 8912896 | tf_op jit(solution)/shard_map/all_gather | solution.py:41
  76.0 147.1 %all-gather.5.cloned.1.call-start = ((), (), s32[]{:S(2)}) async-start(), calls=%async_computation.3 | async-start | bytes 8912896 | tf_op jit(solution)/shard_map/all_gather | solution.py:41
  145.0 0.7 copy-start.6
  152.4 192.0 %all-to-all-start = ((s32[128,1,2]{2,1,0:T(1,128)}), s32[128,1,2]{2,1,0:T(1,128)S(1)}, u32[]{:S(2)}, u32[]{:S(2)}) async-start(s32[128,1,2]{2,1,0:T(1,128)} %bitcast.26), calls=%async_computation | async-start | bytes 131072 | tf_op jit(solution)/shard_map/all_to_all | solution.py:86
  344.4 9.2 %copy-start.3 = (f32[512,256]{1,0:T(8,128)S(1)}, f32[512,256]{1,0:T(8,128)}, u32[]{:S(2)}) copy-start(f32[512,256]{1,0:T(8,128)} %slice.133) | copy-start | bytes 1572868
  344.4 9.2 %copy-start.4 = (f32[512,256]{1,0:T(8,128)S(1)}, f32[512,256]{1,0:T(8,128)}, u32[]{:S(2)}) copy-start(f32[512,256]{1,0:T(8,128)} %fusion.12) | copy-start | bytes 1572868
  344.4 10.4 %copy-start.5 = (f32[256,256]{1,0:T(8,128)S(1)}, f32[256,256]{1,0:T(8,128)}, u32[]{:S(2)}) copy-start(f32[256,256]{1,0:T(8,128)} %get-tuple-element.51) | copy-start | bytes 786436
  344.4 264.6 %all-to-all-start.1 = ((f32[128,2,16384]{2,1,0:T(2,128)}), f32[128,2,16384]{2,1,0:T(2,128)}, u32[]{:S(2)}, u32[]{:S(2)}) async-start(f32[128,2,16384]{2,1,0:T(2,128)} %reshape.216), calls=%async_computation.1 | async-start | bytes 33554432 | tf_op jit(solution)/shard_map/all_to_all | solution.py:85
  629.5 33.5 %copy-start.1 = (s32[1,160,128]{2,1,0:T(8,128)S(1)}, s32[1,160,128]{2,1,0:T(8,128)}, u32[]{:S(2)}) copy-start(s32[1,160,128]{2,1,0:T(8,128)} %param.12) | copy-start | bytes 245764
Sparse Core Ops, SparseCore 0:
  76.1 73.0 all-gather.2
  151.9 71.1 all-gather.4
where the time goes:
time: 680 us; the launch traced here: 670 us
  waiting for transfers between devices  291 us (43%)
  matrix products  124 us (18%)
  other arithmetic  115 us (17%)
  local copies, waits for them, and re-layouts  94 us (14%)
  starting transfers between devices  20.1 us (3%)
  between operations  17.6 us (3%)
  loops' own time  8.6 us (1%)
    all_to_all x1, waiting for transfers between devices, body(): lax.all_to_all(outgoing, ('front', 'grid'), split_axis=0, concat_axis=0,...  252 us
    dot_general x2, matrix products, subtract_outer(): jnp.einsum('rk,ck->rc', left_rows, piece, precision=precise)  60.6 us
    all_gather x2, waiting for transfers between devices, body(): lax.all_gather(panel_cols, 'grid', axis=0, tiled=True)  39.6 us
    reshape x2, local copies, waits for them, and re-layouts, body(): arrived = arrived.reshape(devices * capacity, BLK * BLK)  38 us
    another operation x7, other arithmetic, factor_panels(): second_factor = jnp.linalg.cholesky(updated_pivot)  34.6 us
    another operation x6, other arithmetic, factor_panels(): first_factor = jnp.linalg.cholesky(corner[:NB, :NB])  34 us
    dot_general x1, matrix products, body(): moved = jnp.einsum('qrs,qsx->qrx', permuter, picked, precision=precise)  26.6 us
    unnamed x23, local copies, waits for them, and re-layouts  21.7 us
  transfers between devices with their start and end apart: 4, of which 2 were waited for; matrix products, arithmetic and copies ran while one was open for 32% of the time, Pallas kernels for 0%

commit v1 on v0

--- a/solution.py
+++ b/solution.py
@@ -38,7 +38,12 @@
     for column_start in (0, NB):
         panel_cols = border_factor[:, column_start : column_start + NB]
         schur_rows = subtract_outer(
-            schur_rows, panel_cols, lax.all_gather(panel_cols, "grid", axis=0, tiled=True)
+            schur_rows,
+            panel_cols,
+            jnp.concatenate(
+                lax.all_to_all(jnp.stack([panel_cols] * lax.axis_size("grid")), "grid", 0, 0),
+                axis=0,
+            ),
         )
     group_size = lax.axis_size("grid")
     member = lax.axis_index("grid")

time: 680 us -> 800 us (1.18)
  waiting for transfers between devices: 291 us -> 384 us
  starting transfers between devices: 20.1 us -> 43 us
  between operations: 17.6 us -> 4.2 us
  other arithmetic: 115 us -> 125 us
  local copies, waits for them, and re-layouts: 94 us -> 103 us
  loops' own time: 8.6 us -> 0.36 us
    all_to_all x0 -> x2, waiting for transfers between devices: none -> 133 us  [body(): lax.all_to_all(jnp.stack([panel_cols] * lax.axis_size('grid')), 'grid', 0...]
    all_gather x2 -> x0, waiting for transfers between devices: 39.6 us -> none  [body(): lax.all_gather(panel_cols, 'grid', axis=0, tiled=True)]
    all_to_all x0 -> x2, starting transfers between devices: none -> 16.4 us  [body(): lax.all_to_all(jnp.stack([panel_cols] * lax.axis_size('grid')), 'grid', 0...]
    another operation x2, other arithmetic: 19.7 us -> 29.7 us  [factor_panels(): jax.scipy.linalg.solve_triangular(second_factor, updated_border.T, lower=...]
    another operation x1, loops' own time: 8.29 us -> 0.05 us  [factor_panels(): jax.scipy.linalg.solve_triangular(second_factor, updated_border.T, lower=...]
    another operation x17 -> x19, local copies, waits for them, and re-layouts: 7.95 us -> 15.9 us  [the longest x2 8.05 us: body(): jnp.stack([panel_cols] * lax.axis_size('grid'))]
  transfers between devices with their start and end apart: 4 -> 4, of which waited for: 2 -> 3; matrix products, arithmetic and copies ran while one was open for 32% -> 29% of each run, Pallas kernels for 0% -> 0%
where the time goes in v1:
time: 800 us; the launch traced here: 790 us
  waiting for transfers between devices  384 us (48%)
  matrix products  131 us (16%)
  other arithmetic  125 us (16%)
  local copies, waits for them, and re-layouts  103 us (13%)
  starting transfers between devices  43 us (5%)
    all_to_all x1, waiting for transfers between devices, body(): lax.all_to_all(outgoing, ('front', 'grid'), split_axis=0, concat_axis=0,...  252 us
    all_to_all x2, waiting for transfers between devices, body(): lax.all_to_all(jnp.stack([panel_cols] * lax.axis_size('grid')), 'grid', 0...  133 us
    dot_general x2, matrix products, subtract_outer(): jnp.einsum('rk,ck->rc', left_rows, piece, precision=precise)  60.4 us
    reshape x2, local copies, waits for them, and re-layouts, body(): arrived = arrived.reshape(devices * capacity, BLK * BLK)  38 us
    another operation x7, other arithmetic, factor_panels(): second_factor = jnp.linalg.cholesky(updated_pivot)  34.6 us
    another operation x6, other arithmetic, factor_panels(): first_factor = jnp.linalg.cholesky(corner[:NB, :NB])  34 us
    another operation x2, other arithmetic, factor_panels(): jax.scipy.linalg.solve_triangular(second_factor, updated_border.T, lower=...  29.7 us
    dot_general x1, matrix products, body(): moved = jnp.einsum('qrs,qsx->qrx', permuter, picked, precision=precise)  26.6 us
  transfers between devices with their start and end apart: 4, of which 3 were waited for; matrix products, arithmetic and copies ran while one was open for 29% of the time, Pallas kernels for 0%

profile of v1, /device:TPU:5, one launch (start us, length us, event | category | flops | bytes accessed | tf_op | source)
XLA Modules:
  0.0 790.5 jit_solution(1988943567327341436)
XLA Ops:
  0.7 1.6 copy.53
  2.3 0.7 fusion.61
  3.2 11.7 %cholesky.130 = f32[128,128]{1,0:T(8,128)S(1)} custom-call(f32[128,128]{1,0:T(8,128)S(1)} %cholesky.194), custom_call_target="Cholesky" | custom-call | tf_op jit(solution)/shard_map/jit(cholesky)/cholesky | solution.py:13
  14.9 9.8 %custom-call.19 = f32[1,128,128]{1,2,0:T(8,128)S(1)} custom-call(f32[1,128,128]{2,1,0:T(8,128)S(1)} %get-tuple-element.65), custom_call_target="InvertDiagBlocksLowerTriangular" | custom-call | tf_op jit(solution)/shard_map/jit(cholesky)/cholesky | solution.py:13
  25.3 11.7 %cholesky.147 = f32[128,128]{1,0:T(8,128)S(1)} custom-call(f32[128,128]{1,0:T(8,128)S(1)} %convolution_subtract_fusion.5), custom_call_target="Cholesky" | custom-call | tf_op jit(solution)/shard_map/jit(cholesky)/cholesky | solution.py:13
  37.0 0.6 compare_reduce_fusion.2
  39.0 0.7 fusion.20
  39.8 4.1 while.2
  40.1 0.6 fusion.76
  40.6 1.3 bitcast_dynamic-update-slice_fusion.4
  42.0 0.6 fusion.76
  42.6 1.3 bitcast_dynamic-update-slice_fusion.4
  43.9 19.7 %custom-call.16 = f32[2,128,128]{1,2,0:T(8,128)S(1)} custom-call(f32[2,128,128]{2,1,0:T(8,128)S(1)} %get-tuple-element.11), custom_call_target="InvertDiagBlocksLowerTriangular" | custom-call | tf_op jit(solution)/shard_map/jit(_solve_triangular)/triangular_solve | solution.py:15
  63.6 1.6 copy.55
  65.2 1.0 maximum_bitcast_fusion.1
  66.2 0.5 fusion.13
  66.7 2.1 convolution_subtract_fusion.1
  68.9 1.8 fusion.37
  70.9 4.0 stack.4
  74.9 6.9 all-to-all-start.1
  81.8 1.1 convolution_subtract_fusion.3
  82.9 1.1 copy.59
  84.0 1.0 fusion.17
  85.0 11.7 %cholesky.164 = f32[128,128]{1,0:T(8,128)S(1)} custom-call(f32[128,128]{1,0:T(8,128)S(1)} %cholesky.197), custom_call_target="Cholesky" | custom-call | tf_op jit(solution)/shard_map/jit(cholesky)/cholesky | solution.py:20
  96.7 9.8 %custom-call.20 = f32[1,128,128]{1,2,0:T(8,128)S(1)} custom-call(f32[1,128,128]{2,1,0:T(8,128)S(1)} %get-tuple-element.61), custom_call_target="InvertDiagBlocksLowerTriangular" | custom-call | tf_op jit(solution)/shard_map/jit(cholesky)/cholesky | solution.py:20
  107.3 11.7 %cholesky.181 = f32[128,128]{1,0:T(8,128)S(1)} custom-call(f32[128,128]{1,0:T(8,128)S(1)} %convolution_subtract_fusion.4), custom_call_target="Cholesky" | custom-call | tf_op jit(solution)/shard_map/jit(cholesky)/cholesky | solution.py:20
  119.0 0.6 compare_reduce_fusion
  119.7 0.6 compare_reduce_fusion.1
  121.6 0.7 fusion.19
  122.4 4.0 while.3
  122.4 0.6 fusion.77
  123.0 1.4 bitcast_dynamic-update-slice_fusion.5
  124.4 0.6 fusion.77
  124.9 1.4 bitcast_dynamic-update-slice_fusion.5
  126.3 29.0 %custom-call.17 = f32[2,128,128]{1,2,0:T(8,128)} custom-call(f32[2,128,128]{2,1,0:T(8,128)S(1)} %get-tuple-element.19), custom_call_target="InvertDiagBlocksLowerTriangular" | custom-call | tf_op jit(solution)/shard_map/jit(_solve_triangular)/triangular_solve | solution.py:21
  155.3 0.6 fusion.10
  156.0 0.8 copy-done.3
  156.8 1.3 fusion.15
  158.2 1.3 convolution_subtract_fusion.2
  159.5 1.4 fusion.33
  161.0 39.9 %all-to-all-done.1 = f32[16,512,256]{2,1,0:T(8,128)} async-done(((f32[16,512,256]{2,1,0:T(8,128)}), f32[16,512,256]{2,1,0:T(8,128)}, u32[]{:S(2)}, u32[]{:S(2)}) %all-to-all-start.1) | async-done | bytes 8388640 | tf_op jit(solution)/shard_map/all_to_all | solution.py:44
  200.8 4.0 stack.5
  204.8 9.5 %all-to-all-start.2 = ((f32[16,512,256]{2,1,0:T(8,128)}), f32[16,512,256]{2,1,0:T(8,128)}, u32[]{:S(2)}, u32[]{:S(2)}) async-start(f32[16,512,256]{2,1,0:T(8,128)} %stack.5), calls=%async_computation.2 | async-start | bytes 16777216 | tf_op jit(solution)/shard_map/all_to_all | solution.py:44
  215.5 0.7 gather_fusion.1
  216.3 1.9 gather_fusion
  218.3 0.8 select_n.78
  219.6 18.5 %fusion.56 = f32[512,8192]{1,0:T(8,128)} fusion(f32[8192,256]{1,0:T(8,128)} %bitcast.33, f32[768,256]{1,0:T(8,128)S(1)} %maximum_bitcast_fusion.2), kind=kOutput, calls=%fused_computation.134 | convolution fusion | flops 12884901888 | bytes 25690112 | tf_op jit(solution)/shard_map/rk,ck->rc/dot_general | solution.py:31
  238.1 92.8 %all-to-all-done.2 = f32[16,512,256]{2,1,0:T(8,128)} async-done(((f32[16,512,256]{2,1,0:T(8,128)}), f32[16,512,256]{2,1,0:T(8,128)}, u32[]{:S(2)}, u32[]{:S(2)}) %all-to-all-start.2) | async-done | bytes 8388640 | tf_op jit(solution)/shard_map/all_to_all | solution.py:44
  330.9 15.9 %all-to-all-start = ((s32[128,1,2]{2,1,0:T(1,128)}), s32[128,1,2]{2,1,0:T(1,128)S(1)}, u32[]{:S(2)}, u32[]{:S(2)}) async-start(s32[128,1,2]{2,1,0:T(1,128)} %bitcast.26), calls=%async_computation | async-start | bytes 131072 | tf_op jit(solution)/shard_map/all_to_all | solution.py:91
  346.8 41.9 %fusion.3 = f32[64,8,64,128]{3,1,2,0:T(8,128)} fusion(f32[512,8192]{1,0:T(8,128)} %fusion.56, f32[1,512,8192]{2,1,0:T(8,128)} %param.9, f32[8192,256]{1,0:T(8,128)} %bitcast.34, f32[128,512]{0,1:T(8,128)S(1)} %fusion.33, f32[128,512]{0,1:T(8,128)S(1)} %copy.62), kind=kOutput, calls=%fused_computation.10 | convolution fusion | flops 12893421568 | bytes 59244544 | tf_op jit(solution)/shard_map/rk,ck->rc/dot_general | solution.py:31
  388.7 14.1 %copy.76 = f32[64,8,64,128]{3,2,1,0:T(8,128)} copy(f32[64,8,64,128]{3,1,2,0:T(8,128)} %fusion.3) | data formatting | bytes 33554432
  402.9 20.7 %fusion.6 = f32[256,128,128]{2,0,1:T(8,128)S(1)} fusion(f32[256,4,64,1]{0,2,3,1:T(8,128)S(1)} %bitcast.142, f32[4,128,64,128]{3,2,1,0:T(8,128)} %bitcast.132), kind=kOutput, calls=%fused_computation.14 | convolution fusion | flops 12884901888 | bytes 33816576 | tf_op jit(solution)/shard_map/qkc,krcs->qrs/dot_general | solution.py:81
  423.6 26.6 %fusion.4 = f32[256,128,128]{2,1,0:T(8,128)} fusion(f32[256,128,128]{2,0,1:T(8,128)S(1)} %fusion.6, s32[256,128]{1,0:T(8,128)S(1)} %gather_fusion.1), kind=kOutput, calls=%fused_computation.11 | convolution fusion | flops 6446645248 | bytes 33685504 | tf_op jit(solution)/shard_map/qrs,qsx->qrx/dot_general | solution.py:86
  450.2 19.8 %reshape.228 = f32[128,2,16384]{2,1,0:T(2,128)} reshape(f32[256,128,128]{2,1,0:T(8,128)} %fusion.4) | data formatting | bytes 33554432 | tf_op jit(solution)/shard_map/reshape | solution.py:87
  469.9 10.7 %all-to-all-start.3 = ((f32[128,2,16384]{2,1,0:T(2,128)}), f32[128,2,16384]{2,1,0:T(2,128)}, u32[]{:S(2)}, u32[]{:S(2)}) async-start(f32[128,2,16384]{2,1,0:T(2,128)} %reshape.228), calls=%async_computation.3 | async-start | bytes 33554432 | tf_op jit(solution)/shard_map/all_to_all | solution.py:90
  480.7 1.1 maximum_bitcast_fusion
  481.8 1.1 fusion.11
  482.9 0.5 broadcast.394
  483.4 0.8 reduce.13
  484.3 251.7 %all-to-all-done.3 = f32[128,2,16384]{2,1,0:T(2,128)} async-done(((f32[128,2,16384]{2,1,0:T(2,128)}), f32[128,2,16384]{2,1,0:T(2,128)}, u32[]{:S(2)}, u32[]{:S(2)}) %all-to-all-start.3) | async-done | bytes 16777248 | tf_op jit(solution)/shard_map/all_to_all | solution.py:90
  736.1 20.5 %reshape.229 = f32[256,16384]{1,0:T(8,128)} reshape(f32[128,2,16384]{2,1,0:T(2,128)} %all-to-all-done.3) | data formatting | bytes 33554432 | tf_op jit(solution)/shard_map/reshape | solution.py:93
  756.6 17.5 %copy.69 = f32[256,16384]{0,1:T(8,128)} copy(f32[256,16384]{1,0:T(8,128)} %reshape.229) | data formatting | bytes 33554432 | tf_op jit(solution)/shard_map/reshape | solution.py:93
  774.1 11.4 %fusion.43 = f32[64,128,128]{2,0,1:T(8,128)S(1)} fusion(f32[128,128,256]{2,1,0:T(8,128)} %bitcast.131, s32[256]{0:T(256)S(1)} %eq.86), kind=kOutput, calls=%fused_computation.86 | convolution fusion | flops 3221241856 | bytes 20972544 | tf_op jit(solution)/shard_map/rs,rx->sx/dot_general | solution.py:96
  785.6 4.4 copy.70
  (72 shorter events, 4.0 us)
Async XLA Ops:
  0.6 214.9 %copy-start = (s32[1,160,128]{2,1,0:T(8,128)S(1)}, s32[1,160,128]{2,1,0:T(8,128)}, u32[]{:S(2)}) copy-start(s32[1,160,128]{2,1,0:T(8,128)} %param.12) | copy-start | bytes 245764
  43.9 21.3 %copy-start.4 = (f32[256,256]{1,0:T(8,128)}, f32[256,256]{1,0:T(8,128)S(1)}, u32[]{:S(2)}) copy-start(f32[256,256]{1,0:T(8,128)S(1)} %get-tuple-element.164) | copy-start | bytes 786436
  74.9 125.9 %all-to-all-start.1 = ((f32[16,512,256]{2,1,0:T(8,128)}), f32[16,512,256]{2,1,0:T(8,128)}, u32[]{:S(2)}, u32[]{:S(2)}) async-start(f32[16,512,256]{2,1,0:T(8,128)} %stack.4), calls=%async_computation.1 | async-start | bytes 16777216 | tf_op jit(solution)/shard_map/all_to_all | solution.py:44
  107.0 107.4 %copy-start.7 = (s32[1,160,1]{1,2,0:T(1,128)S(1)}, s32[1,160,1]{1,2,0:T(1,128)}, u32[]{:S(2)}) copy-start(s32[1,160,1]{1,2,0:T(1,128)} %param.10) | copy-start | bytes 1924
  126.3 89.9 %copy-start.2 = (s32[1,160]{1,0:T(1,128)S(1)}, s32[1,160]{1,0:T(1,128)}, u32[]{:S(2)}) copy-start(s32[1,160]{1,0:T(1,128)} %param.11) | copy-start | bytes 1924
  156.0 0.8 copy-start.3
  204.8 126.1 %all-to-all-start.2 = ((f32[16,512,256]{2,1,0:T(8,128)}), f32[16,512,256]{2,1,0:T(8,128)}, u32[]{:S(2)}, u32[]{:S(2)}) async-start(f32[16,512,256]{2,1,0:T(8,128)} %stack.5), calls=%async_computation.2 | async-start | bytes 16777216 | tf_op jit(solution)/shard_map/all_to_all | solution.py:44
  330.9 139.0 %all-to-all-start = ((s32[128,1,2]{2,1,0:T(1,128)}), s32[128,1,2]{2,1,0:T(1,128)S(1)}, u32[]{:S(2)}, u32[]{:S(2)}) async-start(s32[128,1,2]{2,1,0:T(1,128)} %bitcast.26), calls=%async_computation | async-start | bytes 131072 | tf_op jit(solution)/shard_map/all_to_all | solution.py:91
  469.9 11.8 %copy-start.5 = (f32[256,256]{1,0:T(8,128)S(1)}, f32[256,256]{1,0:T(8,128)}, u32[]{:S(2)}) copy-start(f32[256,256]{1,0:T(8,128)} %get-tuple-element.51) | copy-start | bytes 786436
  469.9 11.8 %copy-start.6 = (f32[256,256]{1,0:T(8,128)S(1)}, f32[256,256]{1,0:T(8,128)}, u32[]{:S(2)}) copy-start(f32[256,256]{1,0:T(8,128)} %get-tuple-element.49) | copy-start | bytes 786436
  469.9 266.1 %all-to-all-start.3 = ((f32[128,2,16384]{2,1,0:T(2,128)}), f32[128,2,16384]{2,1,0:T(2,128)}, u32[]{:S(2)}, u32[]{:S(2)}) async-start(f32[128,2,16384]{2,1,0:T(2,128)} %reshape.228), calls=%async_computation.3 | async-start | bytes 33554432 | tf_op jit(solution)/shard_map/all_to_all | solution.py:90
  756.6 33.4 %copy-start.1 = (s32[1,160,128]{2,1,0:T(8,128)S(1)}, s32[1,160,128]{2,1,0:T(8,128)}, u32[]{:S(2)}) copy-start(s32[1,160,128]{2,1,0:T(8,128)} %param.12) | copy-start | bytes 245764
